TPU v7x, 256 devices: a whole 4x4x8 slice. The times are simulated.
256 devices in a mesh: dp: 8 (over z_lo, x), fsdp: 32 (over y, z_hi, core).
Axes of the slice: x: 4, y: 4, z: 8 (z_hi: 4, z_lo: 2; z = z_hi * 2 + z_lo), core: 2. Of those that a mesh axis runs over, the one named last changes fastest.
Arguments:
- glu_out: bfloat16 [256, 768, 1536], P(('dp', 'fsdp')), may hold values from -6 to 6
- residual_in: bfloat16 [256, 768, 1536], P(('dp', 'fsdp')), may hold values from -6 to 6
- cotangent: bfloat16 [256, 768, 1536], P(('dp', 'fsdp')), may hold values from -6 to 6
- lengths: int32 [256], P(('dp', 'fsdp')), may hold values from 192 to 768, as said below
- conv_kernel: bfloat16 [5, 1536], P(None, 'fsdp'), may hold values from -2.5 to 2.5
- norm_gain: bfloat16 [1536], P('fsdp'), may hold values from 0.099609375 to 1.8984375
- norm_bias: bfloat16 [1536], P('fsdp'), may hold values from -3 to 3
- proj_weight: bfloat16 [1536, 1536], P('fsdp'), may hold values from -0.15625 to 0.15625
Outputs:
- block_out: bfloat16 [256, 768, 1536], P(('dp', 'fsdp'))
- glu_grad: bfloat16 [256, 768, 1536], P(('dp', 'fsdp'))
- proj_grad: float32 [1536, 1536], P('fsdp')
- kernel_grad: float32 [5, 1536], P(None, 'fsdp')
- norm_grads: float32 [2, 1536], P(None, 'fsdp')
Inputs may be any that keep to these rules, and one draw needn't show every extreme that they name: `lengths`: lengths are drawn independently for each utterance; one utterance has all 768 frames valid and another has 192.
All inputs are finite; a program needn't handle non-finite values.
Results may differ from a plain program's by a relative error of at most 0.0029.
Values may be sent and summed in bfloat16 or wider, within the bound.
No kernel may reach another device: no remote copies, remote signals or barrier semaphores. Data moves between devices by JAX's collectives and lax.ppermute only.
A program may use at most 128 MiB of HBM per device.

v0:
```python
import jax
import jax.numpy as jnp
from jax import lax
from jax.sharding import PartitionSpec as P

TAPS = 5


def local(glu_out, residual_in, cotangent, lengths, conv_kernel, norm_gain, norm_bias, proj_weight):
    kernel, gain, bias = (
        lax.all_gather(conv_kernel, "fsdp", axis=1, tiled=True),
        lax.all_gather(norm_gain, "fsdp", axis=0, tiled=True),
        lax.all_gather(norm_bias, "fsdp", axis=0, tiled=True),
    )
    kernel = kernel.astype(jnp.float32)
    gain = gain.astype(jnp.float32)
    bias = bias.astype(jnp.float32)
    utt_count, frame_count, width = glu_out.shape
    rows_count = utt_count * frame_count
    half = (TAPS - 1) // 2
    frame_ids = jnp.arange(frame_count, dtype=jnp.int32)
    mask = (frame_ids[None, :] < lengths[:, None]).astype(jnp.float32)[:, :, None]
    masked = glu_out.astype(jnp.float32) * mask
    padded = jnp.pad(masked, ((0, 0), (half, half), (0, 0)))
    conv = jnp.zeros_like(masked)
    for k in range(TAPS):
        conv = conv + kernel[k] * padded[:, k : k + frame_count, :]
    mean_val = jnp.mean(conv, axis=-1, keepdims=True)
    centred = conv - mean_val
    rstd = lax.rsqrt(jnp.mean(centred * centred, axis=-1, keepdims=True) + 1e-05)
    normed = centred * rstd
    pre = normed * gain + bias
    sig = jax.nn.sigmoid(pre)
    swished = (pre * sig).astype(jnp.bfloat16)
    flat = swished.reshape(rows_count, width)
    cols = flat
    proj = jnp.dot(
        cols,
        lax.all_gather(proj_weight, "fsdp", axis=0, tiled=True),
        preferred_element_type=jnp.float32,
    )
    proj = proj.reshape(glu_out.shape)
    block_out = (residual_in.astype(jnp.float32) + mask * proj).astype(jnp.bfloat16)
    gout = (cotangent.astype(jnp.float32) * mask).astype(jnp.bfloat16)
    gflat = gout.reshape(rows_count, width)
    gswish = lax.dot_general(
        gflat,
        lax.all_gather(proj_weight, "fsdp", axis=0, tiled=True),
        (((1,), (1,)), ((), ())),
        preferred_element_type=jnp.float32,
    )
    gswish = gswish.reshape(glu_out.shape)
    gpre = gswish * sig * (1.0 + pre * (1.0 - sig))
    gain_term = jnp.sum(gpre * normed, axis=(0, 1))
    bias_term = jnp.sum(gpre, axis=(0, 1))
    gnorm = gpre * gain
    gconv = rstd * (
        gnorm
        - jnp.mean(gnorm, axis=-1, keepdims=True)
        - normed * jnp.mean(gnorm * normed, axis=-1, keepdims=True)
    )
    kernel_terms = jnp.stack(
        [jnp.sum(gconv * padded[:, k : k + frame_count, :], axis=(0, 1)) for k in range(TAPS)]
    )
    gpad = jnp.pad(gconv, ((0, 0), (half, half), (0, 0)))
    gin = jnp.zeros_like(gconv)
    for k in range(TAPS):
        gin = gin + kernel[k] * gpad[:, TAPS - 1 - k : TAPS - 1 - k + frame_count, :]
    glu_grad = (gin * mask).astype(jnp.bfloat16)
    small = jnp.concatenate([kernel_terms, gain_term[None], bias_term[None]], axis=0)
    small_share = lax.psum_scatter(small, "fsdp", scatter_dimension=1, tiled=True)
    cols = flat
    share = lax.psum_scatter(
        lax.dot_general(cols, gflat, (((0,), (0,)), ((), ())), preferred_element_type=jnp.float32),
        "fsdp",
        scatter_dimension=0,
        tiled=True,
    )
    proj_grad, small_total = lax.psum((share, small_share), "dp")
    return (block_out, glu_grad, proj_grad, small_total[:TAPS], small_total[TAPS:])


def solution(mesh):
    placed = (
        P(("dp", "fsdp"), None, None),
        P(("dp", "fsdp"), None, None),
        P(("dp", "fsdp"), None, None),
        P(("dp", "fsdp")),
        P(None, "fsdp"),
        P("fsdp"),
        P("fsdp"),
        P("fsdp", None),
    )
    return jax.shard_map(
        local,
        mesh=mesh,
        in_specs=placed,
        out_specs=(
            P(("dp", "fsdp"), None, None),
            P(("dp", "fsdp"), None, None),
            P("fsdp", None),
            P(None, "fsdp"),
            P(None, "fsdp"),
        ),
        check_vma=False,
    )
```

profile of v0, /device:TPU:8, one launch (start us, length us, event | category | flops | bytes accessed | tf_op | source)
XLA Modules:
  0.0 451.1 jit_solution(17166549743025896024)
XLA Ops:
  7.2 0.7 all-gather.3.cloned.1.call-update
  8.6 1.3 dynamic-slice
  10.5 0.9 dynamic-update-slice.1
  11.4 0.8 dynamic-update-slice
  12.2 68.2 %all-reduce.4 = (bf16[1536]{0:T(1024)(128)(2,1)S(1)}, bf16[1536]{0:T(1024)(128)(2,1)S(1)}) all-reduce(bf16[1536]{0:T(1024)(128)(2,1)S(1)} %dynamic-update-slice.1, bf16[1536]{0:T(1024)(128)(2,1)S(1)} %dynamic-update-slice), channel_id=1, replica_groups=mesh['dp'=8,'fsdp'=32] {'fsdp'}, use_global_device_ids=true, to_apply=%add.3 | all-reduce | flops 3072 | bytes 12288
  80.5 47.1 %all-gather = bf16[32,48,5]{1,2,0:T(8,128)(2,1)S(1)} all-gather(bf16[1,48,5]{1,2,0:T(8,128)(2,1)} %bitcast.37), channel_id=1, replica_groups=mesh['dp'=8,'fsdp'=32] {'fsdp'}, dimensions={0}, use_global_device_ids=true | all-gather | bytes 15840 | tf_op jit(solution)/shard_map/all_gather | solution.py:11
  127.8 2.0 convert_multiply_fusion
  129.9 3.6 fusion.10
  133.5 0.6 multiply_reduce_fusion.7
  134.2 1.8 copy-done
  135.9 1.0 copy-done.4
  136.9 7.2 %fusion.4 = f32[1536,1536]{1,0:T(8,128)} fusion(bf16[1,768,1536]{2,1,0:T(8,128)(2,1)S(1)} %copy-done.4, f32[768]{0:T(1024)S(1)} %fusion.9, f32[1,768,1536]{2,1,0:T(8,128)S(1)} %get-tuple-element.23, f32[1536]{0:T(1024)S(1)} %convert_element_type.47, f32[1536]{0:T(1024)S(1)} %convert_element_type.46, f32[768]{0:T(1024)S(1)} %add_rsqrt_fusion, ...), kind=kOutput, calls=%fused_computation.28 | convolution fusion | flops 3638034432 | bytes 16536576 | tf_op jit(solution)/shard_map/dot_general | solution.py:74
  144.4 10.1 %multiply_reduce_fusion = (f32[1536]{0:T(1024)S(1)}, f32[768]{0:T(1024)S(1)}, f32[768]{0:T(1024)S(1)}, f32[1536]{0:T(1024)S(1)}, f32[1,768,1536]{2,1,0:T(8,128)S(1)}) fusion(f32[1,768,1536]{2,1,0:T(8,128)} %copy-done, f32[768]{0:T(1024)S(1)} %add_rsqrt_fusion, f32[768]{0:T(1024)S(1)} %broadcast_multiply_fusion.2, f32[1536]{0:T(1024)S(1)} %convert_element_type.46, ...), kind=kOutput, calls=%fused_computation.4 | convolution fusion | flops 3649826304 | bytes 16555008 | tf_op jit(solution)/shard_map/dot_general | solution.py:46
  154.6 17.7 %multiply_reduce_fusion.1 = (f32[1536]{0:T(1024)S(1)}, f32[1536]{0:T(1024)S(1)}, f32[1536]{0:T(1024)S(1)}, f32[1536]{0:T(1024)S(1)}, f32[1536]{0:T(1024)S(1)}, /*index=5*/f32[1,768,1536]{2,1,0:T(8,128)}) fusion(f32[1,768,1536]{2,1,0:T(8,128)} %copy-done.1, f32[768]{0:T(1024)S(1)} %fusion.9, bf16[1,768,1536]{2,1,0:T(8,128)(2,1)S(1)} %copy-done.2, ...), kind=kLoop, calls=%fused_computation.5 | loop fusion | flops 22405632 | bytes 21285888 | tf_op jit(solution)/shard_map/reduce_sum | solution.py:63
  172.4 1.2 copy.16
  173.7 10.8 %fusion.1 = bf16[1,768,1536]{2,1,0:T(8,128)(2,1)} fusion(bf16[1,768,1536]{2,1,0:T(8,128)(2,1)} %param.9, bf16[1536,1536]{1,0:T(8,128)(2,1)} %all-gather.3.cloned.1.call-done, f32[768]{0:T(1024)S(1)} %fusion.9, f32[1,768,1536]{2,1,0:T(8,128)} %copy-done, f32[1536]{0:T(1024)S(1)} %convert_element_type.47, f32[1536]{0:T(1024)S(1)} %convert_element_type.46, ...), kind=kOutput, calls=%fused_computation.3 | convolution fusion | flops 3639214080 | bytes 14177280 | tf_op jit(solution)/shard_map/dot_general | solution.py:37
  184.5 86.9 %reduce-scatter.5.cloned.1.call-done = f32[48,1536]{1,0:T(8,128)} async-done(((f32[1536,1536]{1,0:T(8,128)}), f32[48,1536]{1,0:T(8,128)}) %reduce-scatter.5.cloned.1.call-update) | async-done | bytes 294928 | tf_op jit(solution)/shard_map/reduce_scatter | solution.py:73
  271.4 12.9 %multiply_convert_fusion = bf16[1,768,1536]{2,1,0:T(8,128)(2,1)} fusion(f32[1,768,1536]{2,1,0:T(8,128)} %get-tuple-element.21, f32[1536]{0:T(1024)S(1)} %get-tuple-element.15, f32[1536]{0:T(1024)S(1)} %get-tuple-element.16, f32[1536]{0:T(1024)S(1)} %get-tuple-element.17, f32[1536]{0:T(1024)S(1)} %get-tuple-element.18, f32[768]{0:T(1024)S(1)} %fusion.9, ...), kind=kLoop, calls=%fused_computation.10 | loop fusion | flops 12976128 | bytes 7111680 | tf_op jit(solution)/shard_map/convert_element_type | solution.py:69
  284.3 78.1 %reduce-scatter.7.cloned.1.call-done = f32[48,7]{1,0:T(8,128)} async-done(((f32[1536,7]{1,0:T(8,128)}), f32[48,7]{1,0:T(8,128)}) %reduce-scatter.7.cloned.1.call-update) | async-done | bytes 1360
  362.3 0.8 copy.17
  363.1 18.7 %psum.15 = f32[7,48]{1,0:T(8,128)S(1)} all-reduce(f32[7,48]{1,0:T(8,128)S(1)} %copy.17), channel_id=1, replica_groups=mesh['dp'=8,'fsdp'=32] {'dp'}, use_global_device_ids=true, to_apply=%region_14.15 | all-reduce | flops 336 | bytes 2688 | tf_op jit(solution)/shard_map/psum | solution.py:79
  381.9 0.6 slice.71
  382.4 60.4 %all-reduce.7.cloned.1.call-done = f32[48,1536]{1,0:T(8,128)} async-done(((f32[48,1536]{1,0:T(8,128)}), f32[48,1536]{1,0:T(8,128)}) %all-reduce.7.cloned.1.call-update) | async-done | bytes 294928 | tf_op jit(solution)/shard_map/psum | solution.py:79
  442.8 1.7 copy.23
  (35 shorter events, 0.8 us)
Async XLA Ops:
  7.2 137.3 %all-gather.3.cloned.1.call-start = ((), (), s32[]{:S(2)}) async-start(), calls=%async_computation.2 | async-start | bytes 4866048 | tf_op jit(solution)/shard_map/all_gather | solution.py:39
  7.9 263.5 %reduce-scatter.5.cloned.1.call-start = ((), (), s32[]{:S(2)}) async-start(), calls=%async_computation.3 | async-start | bytes 9732096 | tf_op jit(solution)/shard_map/reduce_scatter | solution.py:73
  129.9 3.6 copy-start.1
  133.5 2.4 copy-start
  133.5 3.4 copy-start.4
  144.2 10.4 %copy-start.2 = (bf16[1,768,1536]{2,1,0:T(8,128)(2,1)S(1)}, bf16[1,768,1536]{2,1,0:T(8,128)(2,1)}, u32[]{:S(2)}) copy-start(bf16[1,768,1536]{2,1,0:T(8,128)(2,1)} %param.8) | copy-start | bytes 7077892
  144.2 218.2 %reduce-scatter.7.cloned.1.call-start = ((), (), s32[]{:S(2)}) async-start(), calls=%async_computation.5 | async-start | bytes 811008
  173.7 269.2 %all-reduce.7.cloned.1.call-start = ((), (), s32[]{:S(2)}) async-start(), calls=%async_computation.4 | async-start | bytes 589824 | tf_op jit(solution)/shard_map/psum | solution.py:79
  381.8 62.7 %copy-start.3 = (f32[7,48]{1,0:T(8,128)}, f32[7,48]{1,0:T(8,128)S(1)}, u32[]{:S(2)}) copy-start(f32[7,48]{1,0:T(8,128)S(1)} %psum.15) | copy-start | bytes 4036
Sparse Core Ops, SparseCore 0:
  10.5 66.0 all-gather.2
  144.3 127.0 reduce-scatter.4
  275.6 86.6 reduce-scatter.6
  365.0 77.7 all-reduce.6
where the time goes:
time: 451 us
  waiting for transfers between devices  226 us (50%)
  blocking collectives  134 us (30%)
  other arithmetic  36.9 us (8%)
  matrix products  28.1 us (6%)
  between operations  15.3 us (3%)
  local copies, waits for them, and re-layouts  10.3 us (2%)
    reduce_scatter x1, waiting for transfers between devices, local(): lax.psum_scatter(lax.dot_general(cols, gflat, (((0,), (0,)), ((), ())), p...  86.9 us
    unnamed x5, waiting for transfers between devices  78.8 us
    unnamed x1, blocking collectives  68.2 us
    psum x1, waiting for transfers between devices, local(): proj_grad, small_total = lax.psum((share, small_share), 'dp')  60.4 us
    all_gather x1, blocking collectives, local(): lax.all_gather(conv_kernel, 'fsdp', axis=1, tiled=True)  47.1 us
    psum x1, blocking collectives, local(): proj_grad, small_total = lax.psum((share, small_share), 'dp')  18.7 us
    reduce_sum x1, other arithmetic, local(): jnp.sum(gconv * padded[:, k:k + frame_count, :], axis=(0, 1))  17.7 us
    convert_element_type x1, other arithmetic, local(): glu_grad = (gin * mask).astype(jnp.bfloat16)  12.9 us
  transfers between devices with their start and end apart: 4, of which 3 were waited for; matrix products, arithmetic and copies ran while one was open for 16% of the time, Pallas kernels for 0%

commit v1 on v0

--- a/solution.py
+++ b/solution.py
@@ -1,3 +1,4 @@
+import functools
 import jax
 import jax.numpy as jnp
 from jax import lax
@@ -6,9 +7,21 @@
 TAPS = 5
 
 
+def extend_racks_over_axis(vec, axis_name):
+    cards = []
+    for _ in range(lax.axis_size(axis_name)):
+        cards.append(vec)
+    e_next = jnp.stack(cards)
+    piece_now = lax.all_to_all(e_next, axis_name, 0, 0)
+    return jnp.concatenate(piece_now, axis=1)
+
+
+ticks_advance = functools.partial(extend_racks_over_axis, axis_name="fsdp")
+
+
 def local(glu_out, residual_in, cotangent, lengths, conv_kernel, norm_gain, norm_bias, proj_weight):
     kernel, gain, bias = (
-        lax.all_gather(conv_kernel, "fsdp", axis=1, tiled=True),
+        ticks_advance(conv_kernel),
         lax.all_gather(norm_gain, "fsdp", axis=0, tiled=True),
         lax.all_gather(norm_bias, "fsdp", axis=0, tiled=True),
     )

time: 451 us -> 429 us (0.951)
  blocking collectives: 134 us -> 86.8 us
  starting transfers between devices: 0.34 us -> 12 us
  other arithmetic: 36.9 us -> 46.2 us
    all_gather x1 -> x0, blocking collectives: 47.1 us -> none  [local(): lax.all_gather(conv_kernel, 'fsdp', axis=1, tiled=True)]
    all_to_all x0 -> x1, starting transfers between devices: none -> 11.7 us  [extend_racks_over_axis(): piece_now = lax.all_to_all(e_next, axis_name, 0, 0)]
    reduce_sum x1, other arithmetic: 3.62 us -> 10.6 us  [local(): mean_val = jnp.mean(conv, axis=-1, keepdims=True)]
    unnamed x18 -> x22, local copies, waits for them, and re-layouts: 9.43 us -> 7.56 us
  transfers between devices with their start and end apart: 4 -> 5, of which waited for: 3 -> 3; matrix products, arithmetic and copies ran while one was open for 16% -> 19% of each run, Pallas kernels for 0% -> 0%
where the time goes in v1:
time: 429 us
  waiting for transfers between devices  230 us (54%)
  blocking collectives  86.8 us (20%)
  other arithmetic  46.2 us (11%)
  matrix products  28.1 us (7%)
  between operations  15.3 us (4%)
  starting transfers between devices  12 us (3%)
  local copies, waits for them, and re-layouts  10.2 us (2%)
    reduce_scatter x1, waiting for transfers between devices, local(): lax.psum_scatter(lax.dot_general(cols, gflat, (((0,), (0,)), ((), ())), p...  90.7 us
    unnamed x5, waiting for transfers between devices  78.9 us
    unnamed x1, blocking collectives  68.1 us
    psum x1, waiting for transfers between devices, local(): proj_grad, small_total = lax.psum((share, small_share), 'dp')  60.4 us
    psum x1, blocking collectives, local(): proj_grad, small_total = lax.psum((share, small_share), 'dp')  18.7 us
    reduce_sum x1, other arithmetic, local(): jnp.sum(gconv * padded[:, k:k + frame_count, :], axis=(0, 1))  17.8 us
    convert_element_type x1, other arithmetic, local(): glu_grad = (gin * mask).astype(jnp.bfloat16)  12.9 us
    all_to_all x1, starting transfers between devices, extend_racks_over_axis(): piece_now = lax.all_to_all(e_next, axis_name, 0, 0)  11.7 us
  transfers between devices with their start and end apart: 5, of which 3 were waited for; matrix products, arithmetic and copies ran while one was open for 19% of the time, Pallas kernels for 0%

profile of v1, /device:TPU:8, one launch (start us, length us, event | category | flops | bytes accessed | tf_op | source)
XLA Modules:
  0.0 428.7 jit_solution(6881206299707910251)
XLA Ops:
  7.2 0.7 all-gather.2.cloned.1.call-update
  7.9 1.3 stack.12
  9.3 11.7 %all-to-all-start = ((bf16[32,5,48]{2,1,0:T(8,128)(2,1)}), bf16[32,5,48]{2,1,0:T(8,128)(2,1)S(1)}, u32[]{:S(2)}, u32[]{:S(2)}) async-start(bf16[32,5,48]{2,1,0:T(8,128)(2,1)} %stack.12), calls=%async_computation | async-start | bytes 131072 | tf_op jit(solution)/shard_map/all_to_all | solution.py:15
  21.7 4.3 convert_multiply_fusion
  26.0 0.6 dynamic-slice
  27.2 0.2 dynamic-update-slice.1
  27.7 68.1 %all-reduce.4 = (bf16[1536]{0:T(1024)(128)(2,1)S(1)}, bf16[1536]{0:T(1024)(128)(2,1)S(1)}) all-reduce(bf16[1536]{0:T(1024)(128)(2,1)S(1)} %dynamic-update-slice.1, bf16[1536]{0:T(1024)(128)(2,1)S(1)} %dynamic-update-slice), channel_id=1, replica_groups=mesh['dp'=8,'fsdp'=32] {'fsdp'}, use_global_device_ids=true, to_apply=%add.3 | all-reduce | flops 3072 | bytes 12288
  96.5 10.6 %fusion.10 = (f32[768]{0:T(1024)S(1)}, f32[1,768,1536]{2,1,0:T(8,128)S(1)}) fusion(f32[1536]{0:T(1024)S(1)} %mul.198, f32[1536]{0:T(1024)S(1)} %mul.195, f32[1,768,1536]{2,1,0:T(8,128)} %convert_multiply_fusion, f32[1536]{0:T(1024)S(1)} %mul.192, f32[1536]{0:T(1024)S(1)} %mul.189, f32[1536]{0:T(1024)S(1)} %mul.184), kind=kLoop, calls=%fused_computation.43 | loop fusion | flops 11795712 | bytes 9470976 | tf_op jit(solution)/shard_map/reduce_sum | solution.py:41
  107.1 0.6 multiply_reduce_fusion.7
  107.7 1.8 copy-done
  109.5 1.0 copy-done.3
  110.5 7.2 %fusion.4 = f32[1536,1536]{1,0:T(8,128)} fusion(bf16[1,768,1536]{2,1,0:T(8,128)(2,1)S(1)} %copy-done.3, f32[768]{0:T(1024)S(1)} %fusion.9, f32[1,768,1536]{2,1,0:T(8,128)S(1)} %get-tuple-element.23, f32[1536]{0:T(1024)S(1)} %convert_element_type.52, f32[1536]{0:T(1024)S(1)} %convert_element_type.51, f32[768]{0:T(1024)S(1)} %add_rsqrt_fusion, ...), kind=kOutput, calls=%fused_computation.28 | convolution fusion | flops 3638034432 | bytes 16536576 | tf_op jit(solution)/shard_map/dot_general | solution.py:87
  118.0 10.1 %multiply_reduce_fusion = (f32[1536]{0:T(1024)S(1)}, f32[768]{0:T(1024)S(1)}, f32[768]{0:T(1024)S(1)}, f32[1536]{0:T(1024)S(1)}, f32[1,768,1536]{2,1,0:T(8,128)S(1)}) fusion(f32[1,768,1536]{2,1,0:T(8,128)} %copy-done, f32[768]{0:T(1024)S(1)} %add_rsqrt_fusion, f32[768]{0:T(1024)S(1)} %broadcast_multiply_fusion.2, f32[1536]{0:T(1024)S(1)} %convert_element_type.51, ...), kind=kOutput, calls=%fused_computation.4 | convolution fusion | flops 3649826304 | bytes 16555008 | tf_op jit(solution)/shard_map/dot_general | solution.py:59
  128.2 17.8 %multiply_reduce_fusion.1 = (f32[1536]{0:T(1024)S(1)}, f32[1536]{0:T(1024)S(1)}, f32[1536]{0:T(1024)S(1)}, f32[1536]{0:T(1024)S(1)}, f32[1536]{0:T(1024)S(1)}, /*index=5*/f32[1,768,1536]{2,1,0:T(8,128)}) fusion(f32[1,768,1536]{2,1,0:T(8,128)} %convert_multiply_fusion, f32[768]{0:T(1024)S(1)} %fusion.9, bf16[1,768,1536]{2,1,0:T(8,128)(2,1)S(1)} %copy-done.1, ...), kind=kLoop, calls=%fused_computation.5 | loop fusion | flops 22405632 | bytes 21285888 | tf_op jit(solution)/shard_map/reduce_sum | solution.py:76
  146.1 1.2 copy.13
  147.4 10.8 %fusion.1 = bf16[1,768,1536]{2,1,0:T(8,128)(2,1)} fusion(bf16[1,768,1536]{2,1,0:T(8,128)(2,1)} %param.9, bf16[1536,1536]{1,0:T(8,128)(2,1)} %all-gather.2.cloned.1.call-done, f32[768]{0:T(1024)S(1)} %fusion.9, f32[1,768,1536]{2,1,0:T(8,128)} %copy-done, f32[1536]{0:T(1024)S(1)} %convert_element_type.52, f32[1536]{0:T(1024)S(1)} %convert_element_type.51, ...), kind=kOutput, calls=%fused_computation.3 | convolution fusion | flops 3639214080 | bytes 14177280 | tf_op jit(solution)/shard_map/dot_general | solution.py:50
  158.2 90.7 %reduce-scatter.5.cloned.1.call-done = f32[48,1536]{1,0:T(8,128)} async-done(((f32[1536,1536]{1,0:T(8,128)}), f32[48,1536]{1,0:T(8,128)}) %reduce-scatter.5.cloned.1.call-update) | async-done | bytes 294928 | tf_op jit(solution)/shard_map/reduce_scatter | solution.py:86
  248.9 12.9 %multiply_convert_fusion = bf16[1,768,1536]{2,1,0:T(8,128)(2,1)} fusion(f32[1,768,1536]{2,1,0:T(8,128)} %get-tuple-element.21, f32[1536]{0:T(1024)S(1)} %mul.198, f32[1536]{0:T(1024)S(1)} %mul.195, f32[1536]{0:T(1024)S(1)} %mul.192, f32[1536]{0:T(1024)S(1)} %mul.189, f32[768]{0:T(1024)S(1)} %fusion.9, f32[1536]{0:T(1024)S(1)} %mul.184), kind=kLoop, calls=%fused_computation.10 | loop fusion | flops 12976128 | bytes 7111680 | tf_op jit(solution)/shard_map/convert_element_type | solution.py:82
  261.8 78.2 %reduce-scatter.7.cloned.1.call-done = f32[48,7]{1,0:T(8,128)} async-done(((f32[1536,7]{1,0:T(8,128)}), f32[48,7]{1,0:T(8,128)}) %reduce-scatter.7.cloned.1.call-update) | async-done | bytes 1360
  340.0 0.8 copy.14
  340.8 18.7 %psum.15 = f32[7,48]{1,0:T(8,128)S(1)} all-reduce(f32[7,48]{1,0:T(8,128)S(1)} %copy.14), channel_id=1, replica_groups=mesh['dp'=8,'fsdp'=32] {'dp'}, use_global_device_ids=true, to_apply=%region_14.15 | all-reduce | flops 336 | bytes 2688 | tf_op jit(solution)/shard_map/psum | solution.py:92
  359.5 0.6 slice.76
  360.1 60.4 %all-reduce.7.cloned.1.call-done = f32[48,1536]{1,0:T(8,128)} async-done(((f32[48,1536]{1,0:T(8,128)}), f32[48,1536]{1,0:T(8,128)}) %all-reduce.7.cloned.1.call-update) | async-done | bytes 294928 | tf_op jit(solution)/shard_map/psum | solution.py:92
  420.5 1.7 copy.19
  (45 shorter events, 1.5 us)
Async XLA Ops:
  7.2 18.8 %copy-start.6 = (u32[256]{0:T(256)S(1)}, u32[256]{0:T(256)}, u32[]{:S(2)}) copy-start(u32[256]{0:T(256)} %constant.28) | copy-start | bytes 3076
  7.2 20.0 %copy-start.4 = (bf16[48]{0:T(256)(128)(2,1)S(1)}, bf16[48]{0:T(256)(128)(2,1)}, u32[]{:S(2)}) copy-start(bf16[48]{0:T(256)(128)(2,1)} %param.14) | copy-start | bytes 292
  7.2 20.3 %copy-start.5 = (bf16[48]{0:T(256)(128)(2,1)S(1)}, bf16[48]{0:T(256)(128)(2,1)}, u32[]{:S(2)}) copy-start(bf16[48]{0:T(256)(128)(2,1)} %param.13) | copy-start | bytes 292
  7.2 110.8 %all-gather.2.cloned.1.call-start = ((), (), s32[]{:S(2)}) async-start(), calls=%async_computation.3 | async-start | bytes 4866048 | tf_op jit(solution)/shard_map/all_gather | solution.py:52
  9.3 86.6 %all-to-all-start = ((bf16[32,5,48]{2,1,0:T(8,128)(2,1)}), bf16[32,5,48]{2,1,0:T(8,128)(2,1)S(1)}, u32[]{:S(2)}, u32[]{:S(2)}) async-start(bf16[32,5,48]{2,1,0:T(8,128)(2,1)} %stack.12), calls=%async_computation | async-start | bytes 131072 | tf_op jit(solution)/shard_map/all_to_all | solution.py:15
  21.0 227.9 %reduce-scatter.5.cloned.1.call-start = ((), (), s32[]{:S(2)}) async-start(), calls=%async_computation.4 | async-start | bytes 9732096 | tf_op jit(solution)/shard_map/reduce_scatter | solution.py:86
  107.1 2.4 copy-start
  107.1 3.4 copy-start.3
  117.7 10.4 %copy-start.1 = (bf16[1,768,1536]{2,1,0:T(8,128)(2,1)S(1)}, bf16[1,768,1536]{2,1,0:T(8,128)(2,1)}, u32[]{:S(2)}) copy-start(bf16[1,768,1536]{2,1,0:T(8,128)(2,1)} %param.8) | copy-start | bytes 7077892
  117.7 222.3 %reduce-scatter.7.cloned.1.call-start = ((), (), s32[]{:S(2)}) async-start(), calls=%async_computation.6 | async-start | bytes 811008
  147.4 273.1 %all-reduce.7.cloned.1.call-start = ((), (), s32[]{:S(2)}) async-start(), calls=%async_computation.5 | async-start | bytes 589824 | tf_op jit(solution)/shard_map/psum | solution.py:92
  359.5 62.6 %copy-start.2 = (f32[7,48]{1,0:T(8,128)}, f32[7,48]{1,0:T(8,128)S(1)}, u32[]{:S(2)}) copy-start(f32[7,48]{1,0:T(8,128)S(1)} %psum.15) | copy-start | bytes 4036
Sparse Core Ops, SparseCore 0:
  10.6 66.0 all-gather.1
  117.8 131.0 reduce-scatter.4
  253.1 86.8 reduce-scatter.6
  342.7 77.7 all-reduce.6
